TPU v7x, 256 devices: a whole 4x4x8 slice. The times are simulated.
256 devices in a mesh: row: 16 (over z, core), col: 16 (over y, x).
Axes of the slice: x: 4, y: 4, z: 8, core: 2. Of those that a mesh axis runs over, the one named last changes fastest.
Arguments:
- matrix: float32 [8192, 8192], P('row', 'col'), as said below
Outputs:
- reduced: float32 [8192, 8192], P('row', 'col')
Inputs may be any that keep to these rules, and one draw needn't show every extreme that they name: matrix is symmetric.
All inputs are finite; a program needn't handle non-finite values.
Results may differ from a plain program's by a relative error of at most 0.00014.
Values sent between devices are 32-bit elements; how exact they have to be, the bound alone decides.
A program may use at most 64 MiB of HBM per device.

v0:
```python
import jax
import jax.numpy as jnp
from jax import lax
from jax.sharding import PartitionSpec as P

BLOCK = 256
PANELS = 2
HIGH = lax.Precision.HIGHEST


def broadcast(block, axis, source):
    block = jnp.where(lax.axis_index(axis) == source, block, jnp.zeros_like(block))
    return lax.psum(block, axis)


def mult(left, right):
    return jnp.dot(left, right, precision=HIGH, preferred_element_type=jnp.float32)


def inverse_transposed(shifted):
    factor = jnp.linalg.cholesky(mult(shifted, shifted.T))
    half = jax.scipy.linalg.solve_triangular(factor, shifted, lower=True)
    return jax.scipy.linalg.solve_triangular(factor, half, lower=True, trans="T")


def reflector_columns(local_rows, column, ratio):
    pieces = broadcast(local_rows, "row", column * ratio + 0)
    return pieces


def update_columns(local_rows, column, ratio):
    pieces = broadcast(local_rows, "row", column * ratio + 0)
    return pieces


def reflect(current, index, row_index, column, ratio):
    height = current.shape[0]
    lead = (index + 1) * BLOCK
    owner = lead // height
    offset_top = lead - owner * height
    rows = row_index * height + jnp.arange(height, dtype=jnp.int32)
    local_panel = jnp.where(
        (rows >= lead)[:, None], current[:, index * BLOCK : (index + 1) * BLOCK], jnp.float32(0.0)
    )
    panel = broadcast(local_panel, "col", 0)
    local_gram = mult(panel.T, panel)
    gram = lax.psum(local_gram, "row")
    top_panel = broadcast(panel[offset_top : offset_top + BLOCK], "row", owner)
    lower = jnp.linalg.cholesky(gram)
    basis = jax.scipy.linalg.solve_triangular(lower, panel.T, lower=True).T
    top = jax.scipy.linalg.solve_triangular(lower, top_panel.T, lower=True).T
    kernel = inverse_transposed(jnp.eye(BLOCK, dtype=jnp.float32) + top)
    unit = ((rows - lead)[:, None] == jnp.arange(BLOCK, dtype=jnp.int32)[None, :]).astype(
        jnp.float32
    )
    vectors = basis + unit
    vectors_cols = reflector_columns(vectors, column, ratio)
    product = lax.psum(mult(current, vectors_cols), "col")
    inner = lax.psum(mult(vectors.T, product), "row")
    coupled = mult(kernel.T, mult(inner, kernel))
    update = mult(product, kernel) - 0.5 * mult(vectors, coupled)
    update_cols = update_columns(update, column, ratio)
    return current - mult(update, vectors_cols.T) - mult(vectors, update_cols.T)


def per_device(matrix):
    row_index = lax.axis_index("row")
    column = lax.axis_index("col")
    ratio = lax.axis_size("row") // lax.axis_size("col")
    current = matrix
    for index in range(PANELS):
        current = reflect(current, index, row_index, column, ratio)
    return current


def solution(mesh):
    in_specs = (P("row", "col"),)
    out_specs = P("row", "col")
    return jax.shard_map(
        per_device, mesh=mesh, in_specs=in_specs, out_specs=out_specs, check_vma=False
    )
```

profile of v0, /device:TPU:1, one launch (start us, length us, event | category | flops | bytes accessed | tf_op | source)
XLA Modules:
  0.0 1581.3 jit_solution(13761343751059832308)
XLA Ops:
  6.5 1.6 copy.8
  9.0 99.1 %all-reduce.16.cloned.1.call-done = f32[512,256]{0,1:T(8,128)} async-done(((f32[512,256]{0,1:T(8,128)}), f32[512,256]{0,1:T(8,128)}) %all-reduce.16.cloned.1.call-update) | async-done | bytes 524304 | tf_op jit(solution)/shard_map/psum | solution.py:13
  108.1 2.5 fusion.90
  110.8 111.6 %all-reduce.18.cloned.1.call-done = f32[256,256]{0,1:T(8,128)} async-done(((f32[256,256]{0,1:T(8,128)}), f32[256,256]{0,1:T(8,128)}) %all-reduce.18.cloned.1.call-update) | async-done | bytes 262160 | tf_op jit(solution)/shard_map/psum | solution.py:47
  223.6 11.7 cholesky.214
  235.3 9.8 custom-call.25
  245.6 11.7 cholesky.231
  259.6 4.3 while.16
  260.4 1.4 bitcast_dynamic-update-slice_fusion.8
  262.4 1.4 bitcast_dynamic-update-slice_fusion.8
  263.9 19.7 %custom-call.26 = f32[2,128,128]{1,2,0:T(8,128)S(1)} custom-call(f32[2,128,128]{2,1,0:T(8,128)S(1)} %get-tuple-element.63), custom_call_target="InvertDiagBlocksLowerTriangular" | custom-call | tf_op jit(solution)/shard_map/jit(_solve_triangular)/triangular_solve | solution.py:50
  285.8 111.3 %all-reduce.20.cloned.1.call-done = f32[512,256]{0,1:T(8,128)} async-done(((f32[512,256]{0,1:T(8,128)}), f32[512,256]{0,1:T(8,128)}) %all-reduce.20.cloned.1.call-update) | async-done | bytes 524304 | tf_op jit(solution)/shard_map/psum | solution.py:13
  397.1 2.9 convolution_bitcast_fusion
  400.8 93.6 %all-reduce.22.cloned.1.call-done = f32[512,256]{0,1:T(8,128)} async-done(((f32[512,256]{0,1:T(8,128)}), f32[512,256]{0,1:T(8,128)}) %all-reduce.22.cloned.1.call-update) | async-done | bytes 524304 | tf_op jit(solution)/shard_map/psum | solution.py:58
  494.4 2.4 fusion.66
  496.8 112.6 %all-reduce.38.cloned.1.call-done = (f32[256,256]{1,0:T(8,128)}, f32[256,256]{1,0:T(8,128)}) async-done(((f32[256,256]{1,0:T(8,128)}, f32[256,256]{1,0:T(8,128)}), (f32[256,256]{1,0:T(8,128)}, f32[256,256]{1,0:T(8,128)})) %all-reduce.38.cloned.1.call-update) | async-done | bytes 524304 | tf_op jit(solution)/shard_map/psum | solution.py:13
  612.2 11.7 cholesky.248
  624.0 9.8 custom-call.28
  634.3 11.7 cholesky.265
  648.6 4.4 while.17
  653.0 19.7 %custom-call.30 = f32[2,128,128]{1,2,0:T(8,128)S(1)} custom-call(f32[2,128,128]{2,1,0:T(8,128)S(1)} %get-tuple-element.66), custom_call_target="InvertDiagBlocksLowerTriangular" | custom-call | tf_op jit(solution)/shard_map/jit(_solve_triangular)/triangular_solve | solution.py:23
  677.4 1.7 broadcast_select_fusion.1
  680.1 2.1 convolution_subtract_fusion.3
  682.2 108.2 %all-reduce.24.cloned.1.call-done = f32[512,256]{0,1:T(8,128)} async-done(((f32[512,256]{0,1:T(8,128)}), f32[512,256]{0,1:T(8,128)}) %all-reduce.24.cloned.1.call-update) | async-done | bytes 524304 | tf_op jit(solution)/shard_map/psum | solution.py:13
  790.4 2.2 convolution_subtract_fusion.2
  793.5 94.3 %all-reduce.26.cloned.1.call-done = f32[512,256]{0,1:T(8,128)} async-done(((f32[512,256]{0,1:T(8,128)}), f32[512,256]{0,1:T(8,128)}) %all-reduce.26.cloned.1.call-update) | async-done | bytes 524304 | tf_op jit(solution)/shard_map/psum | solution.py:13
  887.9 2.5 fusion.91
  890.6 111.4 %all-reduce.28.cloned.1.call-done = f32[256,256]{0,1:T(8,128)} async-done(((f32[256,256]{0,1:T(8,128)}), f32[256,256]{0,1:T(8,128)}) %all-reduce.28.cloned.1.call-update) | async-done | bytes 262160 | tf_op jit(solution)/shard_map/psum | solution.py:47
  1003.3 11.7 cholesky.282
  1015.1 9.8 custom-call.31
  1025.3 11.7 cholesky.299
  1039.9 4.1 while.18
  1040.5 1.4 bitcast_dynamic-update-slice_fusion.10
  1044.0 19.7 %custom-call.32 = f32[2,128,128]{1,2,0:T(8,128)S(1)} custom-call(f32[2,128,128]{2,1,0:T(8,128)S(1)} %get-tuple-element.67), custom_call_target="InvertDiagBlocksLowerTriangular" | custom-call | tf_op jit(solution)/shard_map/jit(_solve_triangular)/triangular_solve | solution.py:50
  1065.9 111.3 %all-reduce.30.cloned.1.call-done = f32[512,256]{0,1:T(8,128)} async-done(((f32[512,256]{0,1:T(8,128)}), f32[512,256]{0,1:T(8,128)}) %all-reduce.30.cloned.1.call-update) | async-done | bytes 524304 | tf_op jit(solution)/shard_map/psum | solution.py:13
  1177.1 3.6 fusion.92
  1181.6 93.6 %all-reduce.32.cloned.1.call-done = f32[512,256]{1,0:T(8,128)} async-done(((f32[512,256]{1,0:T(8,128)}), f32[512,256]{1,0:T(8,128)}) %all-reduce.32.cloned.1.call-update) | async-done | bytes 524304 | tf_op jit(solution)/shard_map/psum | solution.py:58
  1275.2 2.4 fusion.62
  1278.0 112.2 %all-reduce.36.cloned.1.call-done = (f32[256,256]{1,0:T(8,128)}, f32[256,256]{1,0:T(8,128)}) async-done(((f32[256,256]{1,0:T(8,128)}, f32[256,256]{1,0:T(8,128)}), (f32[256,256]{1,0:T(8,128)}, f32[256,256]{1,0:T(8,128)})) %all-reduce.36.cloned.1.call-update) | async-done | bytes 524304 | tf_op jit(solution)/shard_map/psum | solution.py:13
  1393.0 11.7 cholesky.316
  1404.8 9.8 custom-call.34
  1415.1 11.7 cholesky.333
  1429.5 4.1 while.19
  1433.6 19.7 %custom-call.36 = f32[2,128,128]{1,2,0:T(8,128)S(1)} custom-call(f32[2,128,128]{2,1,0:T(8,128)S(1)} %get-tuple-element.70), custom_call_target="InvertDiagBlocksLowerTriangular" | custom-call | tf_op jit(solution)/shard_map/jit(_solve_triangular)/triangular_solve | solution.py:23
  1458.0 1.7 broadcast_select_fusion
  1460.7 2.1 convolution_subtract_fusion.1
  1462.8 108.0 %all-reduce.34.cloned.1.call-done = f32[512,256]{0,1:T(8,128)} async-done(((f32[512,256]{0,1:T(8,128)}), f32[512,256]{0,1:T(8,128)}) %all-reduce.34.cloned.1.call-update) | async-done | bytes 524304 | tf_op jit(solution)/shard_map/psum | solution.py:13
  1570.8 2.2 convolution_subtract_fusion
  (165 shorter events, 47.6 us)
Async XLA Ops:
  6.5 101.6 %all-reduce.16.cloned.1.call-start = ((), (), s32[]{:S(2)}) async-start(), calls=%async_computation | async-start | bytes 1048576 | tf_op jit(solution)/shard_map/psum | solution.py:13
  9.0 213.3 %all-reduce.18.cloned.1.call-start = ((), (), s32[]{:S(2)}) async-start(), calls=%async_computation.1 | async-start | bytes 524288 | tf_op jit(solution)/shard_map/psum | solution.py:47
  110.7 286.4 %all-reduce.20.cloned.1.call-start = ((), (), s32[]{:S(2)}) async-start(), calls=%async_computation.2 | async-start | bytes 1048576 | tf_op jit(solution)/shard_map/psum | solution.py:13
  222.3 1.2 copy-start.7
  259.5 24.1 %copy-start = (f32[512,256]{0,1:T(8,128)S(1)}, f32[512,256]{0,1:T(8,128)}, u32[]{:S(2)}) copy-start(f32[512,256]{0,1:T(8,128)} %all-reduce.16.cloned.1.call-done) | copy-start | bytes 1572868
  284.4 112.7 %copy-start.2 = (f32[512,512]{1,0:T(8,128)S(1)}, f32[512,512]{1,0:T(8,128)}, u32[]{:S(2)}) copy-start(f32[512,512]{1,0:T(8,128)} %param.8) | copy-start | bytes 3145732
  285.7 208.6 %all-reduce.22.cloned.1.call-start = ((), (), s32[]{:S(2)}) async-start(), calls=%async_computation.3 | async-start | bytes 1048576 | tf_op jit(solution)/shard_map/psum | solution.py:58
  400.0 209.5 %all-reduce.38.cloned.1.call-start = ((), (), s32[]{:S(2)}) async-start(), calls=%async_computation.11 | async-start | bytes 1048576 | tf_op jit(solution)/shard_map/psum | solution.py:13
  496.8 293.6 %all-reduce.24.cloned.1.call-start = ((), (), s32[]{:S(2)}) async-start(), calls=%async_computation.4 | async-start | bytes 1048576 | tf_op jit(solution)/shard_map/psum | solution.py:13
  609.5 1.3 copy-start.11
  674.3 1.0 copy-start.10
  675.7 1.0 copy-start.4
  679.1 1.0 copy-start.6
  679.1 208.7 %all-reduce.26.cloned.1.call-start = ((), (), s32[]{:S(2)}) async-start(), calls=%async_computation.5 | async-start | bytes 1048576 | tf_op jit(solution)/shard_map/psum | solution.py:13
  793.5 208.6 %all-reduce.28.cloned.1.call-start = ((), (), s32[]{:S(2)}) async-start(), calls=%async_computation.6 | async-start | bytes 524288 | tf_op jit(solution)/shard_map/psum | solution.py:47
  890.4 286.7 %all-reduce.30.cloned.1.call-start = ((), (), s32[]{:S(2)}) async-start(), calls=%async_computation.7 | async-start | bytes 1048576 | tf_op jit(solution)/shard_map/psum | solution.py:13
  1002.0 1.2 copy-start.8
  1039.8 23.9 %copy-start.1 = (f32[512,256]{0,1:T(8,128)S(1)}, f32[512,256]{0,1:T(8,128)}, u32[]{:S(2)}) copy-start(f32[512,256]{0,1:T(8,128)} %all-reduce.26.cloned.1.call-done) | copy-start | bytes 1572868
  1065.8 209.4 %all-reduce.32.cloned.1.call-start = ((), (), s32[]{:S(2)}) async-start(), calls=%async_computation.8 | async-start | bytes 1048576 | tf_op jit(solution)/shard_map/psum | solution.py:58
  1180.8 209.5 %all-reduce.36.cloned.1.call-start = ((), (), s32[]{:S(2)}) async-start(), calls=%async_computation.10 | async-start | bytes 1048576 | tf_op jit(solution)/shard_map/psum | solution.py:13
  1277.6 293.3 %all-reduce.34.cloned.1.call-start = ((), (), s32[]{:S(2)}) async-start(), calls=%async_computation.9 | async-start | bytes 1048576 | tf_op jit(solution)/shard_map/psum | solution.py:13
  1390.3 1.3 copy-start.12
  1454.9 1.0 copy-start.9
  1456.3 1.0 copy-start.3
  1459.7 1.0 copy-start.5
Sparse Core Ops, SparseCore 0:
  10.5 97.5 all-reduce.15
  110.8 111.4 all-reduce.17
  285.8 111.1 all-reduce.19
  400.1 94.1 all-reduce.21
  496.9 112.5 all-reduce.37
  679.2 111.1 all-reduce.23
  793.6 94.1 all-reduce.25
  890.5 111.4 all-reduce.27
  1065.9 111.1 all-reduce.29
  1180.9 94.1 all-reduce.31
  1277.7 112.5 all-reduce.35
  1459.8 110.9 all-reduce.33
where the time goes:
time: 1590 us; the launch traced here: 1580 us
  waiting for transfers between devices  1270 us (80%)
  other arithmetic  222 us (14%)
  matrix products  44.4 us (3%)
  local copies, waits for them, and re-layouts  25.8 us (2%)
  between operations  19.8 us (1%)
    psum x8, waiting for transfers between devices, broadcast(): return lax.psum(block, axis)  857 us
    psum x2, waiting for transfers between devices, reflect(): gram = lax.psum(local_gram, 'row')  223 us
    psum x2, waiting for transfers between devices, reflect(): product = lax.psum(mult(current, vectors_cols), 'col')  187 us
    another operation x14, other arithmetic, inverse_transposed(): factor = jnp.linalg.cholesky(mult(shifted, shifted.T))  69.2 us
    another operation x13, other arithmetic, reflect(): lower = jnp.linalg.cholesky(gram)  68.7 us
    another operation x5, other arithmetic, reflect(): basis = jax.scipy.linalg.solve_triangular(lower, panel.T, lower=True).T  39.4 us
    another operation x4, other arithmetic, inverse_transposed(): jax.scipy.linalg.solve_triangular(factor, half, lower=True, trans='T')  39.4 us
    dot_general x20, matrix products, mult(): jnp.dot(left, right, precision=HIGH, preferred_element_type=jnp.float32)  32.7 us
  transfers between devices with their start and end apart: 12, of which 12 were waited for; matrix products, arithmetic and copies ran while one was open for 0% of the time, Pallas kernels for 0%

commit v1 on v0

--- a/solution.py
+++ b/solution.py
@@ -44,7 +44,7 @@
     )
     panel = broadcast(local_panel, "col", 0)
     local_gram = mult(panel.T, panel)
-    gram = lax.psum(local_gram, "row")
+    gram = jnp.sum(lax.all_gather(local_gram, "row"), axis=0)
     top_panel = broadcast(panel[offset_top : offset_top + BLOCK], "row", owner)
     lower = jnp.linalg.cholesky(gram)
     basis = jax.scipy.linalg.solve_triangular(lower, panel.T, lower=True).T

time: 1590 us -> 1460 us (0.918)
  waiting for transfers between devices: 1270 us -> 1130 us
    psum x2 -> x0, waiting for transfers between devices: 223 us -> none  [reflect(): gram = lax.psum(local_gram, 'row')]
    all_gather x0 -> x2, waiting for transfers between devices: none -> 87.3 us  [reflect(): gram = jnp.sum(lax.all_gather(local_gram, 'row'), axis=0)]
where the time goes in v1:
time: 1460 us; the launch traced here: 1450 us
  waiting for transfers between devices  1130 us (77%)
  other arithmetic  227 us (16%)
  matrix products  48 us (3%)
  between operations  20 us (1%)
  local copies, waits for them, and re-layouts  19.6 us (1%)
    psum x8, waiting for transfers between devices, broadcast(): return lax.psum(block, axis)  855 us
    psum x2, waiting for transfers between devices, reflect(): product = lax.psum(mult(current, vectors_cols), 'col')  187 us
    all_gather x2, waiting for transfers between devices, reflect(): gram = jnp.sum(lax.all_gather(local_gram, 'row'), axis=0)  87.3 us
    another operation x14, other arithmetic, inverse_transposed(): factor = jnp.linalg.cholesky(mult(shifted, shifted.T))  69.2 us
    another operation x13, other arithmetic, reflect(): lower = jnp.linalg.cholesky(gram)  68.7 us
    another operation x5, other arithmetic, reflect(): basis = jax.scipy.linalg.solve_triangular(lower, panel.T, lower=True).T  39.4 us
    another operation x4, other arithmetic, inverse_transposed(): jax.scipy.linalg.solve_triangular(factor, half, lower=True, trans='T')  39.4 us
    dot_general x20, matrix products, mult(): jnp.dot(left, right, precision=HIGH, preferred_element_type=jnp.float32)  34.7 us
  transfers between devices with their start and end apart: 12, of which 12 were waited for; matrix products, arithmetic and copies ran while one was open for 0% of the time, Pallas kernels for 0%

profile of v1, /device:TPU:1, one launch (start us, length us, event | category | flops | bytes accessed | tf_op | source)
XLA Modules:
  0.0 1446.0 jit_solution(5462608233593649379)
XLA Ops:
  6.5 1.6 copy.22
  9.0 99.1 %all-reduce.14.cloned.1.call-done = f32[512,256]{0,1:T(8,128)} async-done(((f32[512,256]{0,1:T(8,128)}), f32[512,256]{0,1:T(8,128)}) %all-reduce.14.cloned.1.call-update) | async-done | bytes 524304 | tf_op jit(solution)/shard_map/psum | solution.py:13
  108.2 2.5 fusion.90
  110.8 43.8 %all-gather.5.cloned.1.call-done = f32[4096,256]{1,0:T(8,128)} async-done(((f32[256,256]{1,0:T(8,128)}), f32[4096,256]{1,0:T(8,128)}) %all-gather.5.cloned.1.call-update) | async-done | bytes 4194320 | tf_op jit(solution)/shard_map/all_gather | solution.py:47
  154.6 2.5 reduce_sum.18
  157.4 11.7 cholesky.214
  169.1 9.8 custom-call.25
  179.4 11.7 cholesky.231
  193.4 4.5 while.16
  194.3 1.4 bitcast_dynamic-update-slice_fusion.8
  197.8 19.7 %custom-call.26 = f32[2,128,128]{1,2,0:T(8,128)S(1)} custom-call(f32[2,128,128]{2,1,0:T(8,128)S(1)} %get-tuple-element.63), custom_call_target="InvertDiagBlocksLowerTriangular" | custom-call | tf_op jit(solution)/shard_map/jit(_solve_triangular)/triangular_solve | solution.py:50
  219.7 108.8 %all-reduce.16.cloned.1.call-done = f32[512,256]{0,1:T(8,128)} async-done(((f32[512,256]{0,1:T(8,128)}), f32[512,256]{0,1:T(8,128)}) %all-reduce.16.cloned.1.call-update) | async-done | bytes 524304 | tf_op jit(solution)/shard_map/psum | solution.py:13
  328.5 2.9 convolution_bitcast_fusion
  332.2 93.6 %all-reduce.18.cloned.1.call-done = f32[512,256]{0,1:T(8,128)} async-done(((f32[512,256]{0,1:T(8,128)}), f32[512,256]{0,1:T(8,128)}) %all-reduce.18.cloned.1.call-update) | async-done | bytes 524304 | tf_op jit(solution)/shard_map/psum | solution.py:58
  425.8 2.4 fusion.66
  428.3 112.6 %all-reduce.32.cloned.1.call-done = (f32[256,256]{1,0:T(8,128)}, f32[256,256]{1,0:T(8,128)}) async-done(((f32[256,256]{1,0:T(8,128)}, f32[256,256]{1,0:T(8,128)}), (f32[256,256]{1,0:T(8,128)}, f32[256,256]{1,0:T(8,128)})) %all-reduce.32.cloned.1.call-update) | async-done | bytes 524304 | tf_op jit(solution)/shard_map/psum | solution.py:13
  544.5 11.7 cholesky.248
  556.3 9.8 custom-call.28
  566.6 11.7 cholesky.265
  580.9 4.1 while.17
  585.1 19.7 %custom-call.30 = f32[2,128,128]{1,2,0:T(8,128)S(1)} custom-call(f32[2,128,128]{2,1,0:T(8,128)S(1)} %get-tuple-element.66), custom_call_target="InvertDiagBlocksLowerTriangular" | custom-call | tf_op jit(solution)/shard_map/jit(_solve_triangular)/triangular_solve | solution.py:23
  609.3 1.7 broadcast_select_fusion.1
  611.1 2.1 convolution_subtract_fusion.3
  613.2 109.1 %all-reduce.20.cloned.1.call-done = f32[512,256]{0,1:T(8,128)} async-done(((f32[512,256]{0,1:T(8,128)}), f32[512,256]{0,1:T(8,128)}) %all-reduce.20.cloned.1.call-update) | async-done | bytes 524304 | tf_op jit(solution)/shard_map/psum | solution.py:13
  722.4 2.2 convolution_subtract_fusion.2
  725.5 94.3 %all-reduce.22.cloned.1.call-done = f32[512,256]{0,1:T(8,128)} async-done(((f32[512,256]{0,1:T(8,128)}), f32[512,256]{0,1:T(8,128)}) %all-reduce.22.cloned.1.call-update) | async-done | bytes 524304 | tf_op jit(solution)/shard_map/psum | solution.py:13
  819.8 2.5 fusion.91
  822.8 43.4 %all-gather.7.cloned.1.call-done = f32[4096,256]{1,0:T(8,128)} async-done(((f32[256,256]{1,0:T(8,128)}), f32[4096,256]{1,0:T(8,128)}) %all-gather.7.cloned.1.call-update) | async-done | bytes 4194320 | tf_op jit(solution)/shard_map/all_gather | solution.py:47
  866.3 2.5 reduce_sum.19
  869.0 11.7 cholesky.282
  880.8 9.8 custom-call.31
  891.1 11.7 cholesky.299
  905.6 4.3 while.18
  909.8 19.7 %custom-call.32 = f32[2,128,128]{1,2,0:T(8,128)S(1)} custom-call(f32[2,128,128]{2,1,0:T(8,128)S(1)} %get-tuple-element.67), custom_call_target="InvertDiagBlocksLowerTriangular" | custom-call | tf_op jit(solution)/shard_map/jit(_solve_triangular)/triangular_solve | solution.py:50
  931.7 109.0 %all-reduce.24.cloned.1.call-done = f32[512,256]{0,1:T(8,128)} async-done(((f32[512,256]{0,1:T(8,128)}), f32[512,256]{0,1:T(8,128)}) %all-reduce.24.cloned.1.call-update) | async-done | bytes 524304 | tf_op jit(solution)/shard_map/psum | solution.py:13
  1040.7 3.6 fusion.92
  1045.2 93.6 %all-reduce.26.cloned.1.call-done = f32[512,256]{1,0:T(8,128)} async-done(((f32[512,256]{1,0:T(8,128)}), f32[512,256]{1,0:T(8,128)}) %all-reduce.26.cloned.1.call-update) | async-done | bytes 524304 | tf_op jit(solution)/shard_map/psum | solution.py:58
  1138.7 2.4 fusion.62
  1141.2 112.6 %all-reduce.30.cloned.1.call-done = (f32[256,256]{1,0:T(8,128)}, f32[256,256]{1,0:T(8,128)}) async-done(((f32[256,256]{1,0:T(8,128)}, f32[256,256]{1,0:T(8,128)}), (f32[256,256]{1,0:T(8,128)}, f32[256,256]{1,0:T(8,128)})) %all-reduce.30.cloned.1.call-update) | async-done | bytes 524304 | tf_op jit(solution)/shard_map/psum | solution.py:13
  1257.4 11.7 cholesky.316
  1269.2 9.8 custom-call.34
  1279.5 11.7 cholesky.333
  1293.9 4.2 while.19
  1298.1 19.7 %custom-call.36 = f32[2,128,128]{1,2,0:T(8,128)S(1)} custom-call(f32[2,128,128]{2,1,0:T(8,128)S(1)} %get-tuple-element.70), custom_call_target="InvertDiagBlocksLowerTriangular" | custom-call | tf_op jit(solution)/shard_map/jit(_solve_triangular)/triangular_solve | solution.py:23
  1322.3 1.7 broadcast_select_fusion
  1324.0 2.1 convolution_subtract_fusion.1
  1326.1 109.2 %all-reduce.28.cloned.1.call-done = f32[512,256]{0,1:T(8,128)} async-done(((f32[512,256]{0,1:T(8,128)}), f32[512,256]{0,1:T(8,128)}) %all-reduce.28.cloned.1.call-update) | async-done | bytes 524304 | tf_op jit(solution)/shard_map/psum | solution.py:13
  1435.3 2.2 convolution_subtract_fusion
  (155 shorter events, 47.6 us)
Async XLA Ops:
  6.5 101.6 %all-reduce.14.cloned.1.call-start = ((), (), s32[]{:S(2)}) async-start(), calls=%async_computation | async-start | bytes 1048576 | tf_op jit(solution)/shard_map/psum | solution.py:13
  9.0 145.6 %all-gather.5.cloned.1.call-start = ((), (), s32[]{:S(2)}) async-start(), calls=%async_computation.8 | async-start | bytes 4456448 | tf_op jit(solution)/shard_map/all_gather | solution.py:47
  110.7 217.8 %all-reduce.16.cloned.1.call-start = ((), (), s32[]{:S(2)}) async-start(), calls=%async_computation.1 | async-start | bytes 1048576 | tf_op jit(solution)/shard_map/psum | solution.py:13
  154.6 62.9 %copy-start = (f32[512,256]{0,1:T(8,128)S(1)}, f32[512,256]{0,1:T(8,128)}, u32[]{:S(2)}) copy-start(f32[512,256]{0,1:T(8,128)} %all-reduce.14.cloned.1.call-done) | copy-start | bytes 1572868
  157.1 171.4 %copy-start.2 = (f32[512,512]{1,0:T(8,128)S(1)}, f32[512,512]{1,0:T(8,128)}, u32[]{:S(2)}) copy-start(f32[512,512]{1,0:T(8,128)} %param.8) | copy-start | bytes 3145732
  219.7 206.2 %all-reduce.18.cloned.1.call-start = ((), (), s32[]{:S(2)}) async-start(), calls=%async_computation.2 | async-start | bytes 1048576 | tf_op jit(solution)/shard_map/psum | solution.py:58
  331.4 209.5 %all-reduce.32.cloned.1.call-start = ((), (), s32[]{:S(2)}) async-start(), calls=%async_computation.11 | async-start | bytes 1048576 | tf_op jit(solution)/shard_map/psum | solution.py:13
  428.2 294.1 %all-reduce.20.cloned.1.call-start = ((), (), s32[]{:S(2)}) async-start(), calls=%async_computation.3 | async-start | bytes 1048576 | tf_op jit(solution)/shard_map/psum | solution.py:13
  544.2 64.4 %copy-start.4 = (f32[512,256]{0,1:T(8,128)S(1)}, f32[512,256]{0,1:T(8,128)}, u32[]{:S(2)}) copy-start(f32[512,256]{0,1:T(8,128)} %all-reduce.18.cloned.1.call-done) | copy-start | bytes 1572868
  585.1 26.0 %copy-start.6 = (f32[512,256]{0,1:T(8,128)S(1)}, f32[512,256]{0,1:T(8,128)}, u32[]{:S(2)}) copy-start(f32[512,256]{0,1:T(8,128)} %all-reduce.16.cloned.1.call-done) | copy-start | bytes 1572868
  611.0 208.8 %all-reduce.22.cloned.1.call-start = ((), (), s32[]{:S(2)}) async-start(), calls=%async_computation.4 | async-start | bytes 1048576 | tf_op jit(solution)/shard_map/psum | solution.py:13
  725.4 140.9 %all-gather.7.cloned.1.call-start = ((), (), s32[]{:S(2)}) async-start(), calls=%async_computation.9 | async-start | bytes 4456448 | tf_op jit(solution)/shard_map/all_gather | solution.py:47
  822.3 218.4 %all-reduce.24.cloned.1.call-start = ((), (), s32[]{:S(2)}) async-start(), calls=%async_computation.5 | async-start | bytes 1048576 | tf_op jit(solution)/shard_map/psum | solution.py:13
  866.3 63.3 %copy-start.1 = (f32[512,256]{0,1:T(8,128)S(1)}, f32[512,256]{0,1:T(8,128)}, u32[]{:S(2)}) copy-start(f32[512,256]{0,1:T(8,128)} %all-reduce.22.cloned.1.call-done) | copy-start | bytes 1572868
  931.7 207.1 %all-reduce.26.cloned.1.call-start = ((), (), s32[]{:S(2)}) async-start(), calls=%async_computation.6 | async-start | bytes 1048576 | tf_op jit(solution)/shard_map/psum | solution.py:58
  1044.4 209.5 %all-reduce.30.cloned.1.call-start = ((), (), s32[]{:S(2)}) async-start(), calls=%async_computation.10 | async-start | bytes 1048576 | tf_op jit(solution)/shard_map/psum | solution.py:13
  1141.2 294.1 %all-reduce.28.cloned.1.call-start = ((), (), s32[]{:S(2)}) async-start(), calls=%async_computation.7 | async-start | bytes 1048576 | tf_op jit(solution)/shard_map/psum | solution.py:13
  1257.2 64.4 %copy-start.3 = (f32[512,256]{1,0:T(8,128)S(1)}, f32[512,256]{1,0:T(8,128)}, u32[]{:S(2)}) copy-start(f32[512,256]{1,0:T(8,128)} %all-reduce.26.cloned.1.call-done) | copy-start | bytes 1572868
  1298.1 25.9 %copy-start.5 = (f32[512,256]{0,1:T(8,128)S(1)}, f32[512,256]{0,1:T(8,128)}, u32[]{:S(2)}) copy-start(f32[512,256]{0,1:T(8,128)} %all-reduce.24.cloned.1.call-done) | copy-start | bytes 1572868
Sparse Core Ops, SparseCore 0:
  10.5 97.5 all-reduce.13
  110.8 43.7 all-gather.4
  219.8 108.7 all-reduce.15
  331.6 94.1 all-reduce.17
  428.4 112.5 all-reduce.31
  611.2 111.1 all-reduce.19
  725.5 94.1 all-reduce.21
  822.5 43.7 all-gather.6
  931.8 108.8 all-reduce.23
  1044.5 94.1 all-reduce.25
  1141.3 112.5 all-reduce.29
  1324.1 111.1 all-reduce.27
